TPU v7x, 128 devices: a whole 4x4x4 slice. The times are simulated.
128 devices in a mesh: blk: 32 (over z_hi, y, x), head: 4 (over z_lo, core).
Axes of the slice: x: 4, y: 4, z: 4 (z_hi: 2, z_lo: 2; z = z_hi * 2 + z_lo), core: 2. Of those that a mesh axis runs over, the one named last changes fastest.
Arguments:
- tokens: bfloat16 [12288, 1024], P(('blk', 'head')), may hold values from -18 to 18
- block_order: int32 [64], replicated, may hold values from 0 to 63, as said below
- request_lengths: int32 [9], replicated, may hold values from 1 to 9216, 12288 in all
- enc_lengths: int32 [9], replicated, may hold values from 1 to 512, 2048 in all
- w_qkv: bfloat16 [3, 1024, 1024], P(None, None, 'head'), may hold values from -0.1875 to 0.1875
- w_out: bfloat16 [1024, 1024], P('head'), may hold values from -0.1875 to 0.1875
- enc_kv: bfloat16 [2, 2048, 1024], P(None, 'blk', 'head'), may hold values from -18 to 18
- w_cq: bfloat16 [1024, 1024], replicated, may hold values from -0.1875 to 0.1875
- w_co: bfloat16 [1024, 1024], replicated, may hold values from -0.1875 to 0.1875
- w_up: bfloat16 [1024, 4096], replicated, may hold values from -0.1875 to 0.1875
- w_down: bfloat16 [4096, 1024], replicated, may hold values from -0.09375 to 0.09375
- w_next: bfloat16 [3, 1024, 1024], P(None, None, 'head'), may hold values from -0.1875 to 0.1875
Outputs:
- output: float32 [12288, 1024], P(('blk', 'head'))
- cache: bfloat16 [2, 12288, 1024], P(None, 'blk', 'head')
- next_qkv: float32 [3, 12288, 1024], P(None, 'blk', 'head')
Inputs may be any that keep to these rules, and one draw needn't show every extreme that they name: `block_order`: each half-block index appears once, and stored half-blocks 2i and 2i + 1 hold position blocks that add up to 63. `request_lengths`: the lengths sum to 12288. `enc_lengths`: the lengths sum to 2048.
All inputs are finite; a program needn't handle non-finite values.
Results may differ from a plain program's by a relative error of at most 0.024.
Values may be sent and summed in bfloat16 or wider, within the bound.
A program may use at most 128 MiB of HBM per device.

v0:
```python
import math
import jax
import jax.numpy as jnp
from jax import lax
from jax.sharding import PartitionSpec as P

HEADS = 16
NEGATIVE = -1e30
SCALING = 0.125
EPSILON = 1e-05


def normalize(matrix):
    center = matrix - jnp.mean(matrix, axis=-1, keepdims=True)
    return center * lax.rsqrt(jnp.mean(center * center, axis=-1, keepdims=True) + EPSILON)


def position_of(order_table, indices, halfway):
    slots = jnp.arange(order_table.shape[0], dtype=jnp.int32)
    picked = jnp.sum(
        jnp.where((indices // halfway)[:, None] == slots[None, :], order_table[None, :], 0), axis=1
    )
    return picked * halfway + indices % halfway


def group_of(places, lengths):
    ends = jnp.cumsum(lengths)
    return jnp.sum((places[:, None] >= ends[None, :]).astype(jnp.int32), axis=1)


def online_update(carried, queries, key_rows, value_rows, visible):
    maxima, totals, running = carried
    heads_here = queries.shape[1]
    key_split = key_rows.reshape(key_rows.shape[0], heads_here, -1)
    value_split = value_rows.reshape(value_rows.shape[0], heads_here, -1)
    scores = (
        jnp.einsum("qhd,khd->qhk", queries, key_split, preferred_element_type=jnp.float32) * SCALING
    )
    scores = jnp.where(visible[:, None, :], scores, NEGATIVE)
    updated = jnp.maximum(maxima, jnp.max(scores, axis=2))
    factor = jnp.exp(maxima - updated)
    weights = jnp.exp(scores - updated[:, :, None])
    totals = totals * factor + jnp.sum(weights, axis=2)
    running = running * factor[:, :, None] + jnp.einsum(
        "qhk,khd->qhd",
        weights.astype(jnp.bfloat16),
        value_split,
        preferred_element_type=jnp.float32,
    )
    return (updated, totals, running)


def sweep(
    carried, queries, key_rows, value_rows, key_places, key_groups, query_places, query_groups
):
    length = key_rows.shape[0]
    block_size = math.gcd(length, 2048)
    blocks_count = length // block_size
    key_blocks = key_rows.reshape(blocks_count, block_size, key_rows.shape[1])
    value_blocks = value_rows.reshape(blocks_count, block_size, value_rows.shape[1])
    group_blocks = key_groups.reshape(blocks_count, block_size)
    if key_places is None:
        place_blocks = group_blocks
    else:
        place_blocks = key_places.reshape(blocks_count, block_size)

    def advance(status, element):
        key_block, value_block, place_block, group_block = element
        visible = group_block[None, :] == query_groups[:, None]
        if key_places is None:
            return (online_update(status, queries, key_block, value_block, visible), None)
        visible = visible & (place_block[None, :] <= query_places[:, None])
        updated = online_update(status, queries, key_block, value_block, visible)
        return (updated, None)

    carried, unused = lax.scan(
        advance, carried, (key_blocks, value_blocks, place_blocks, group_blocks)
    )
    return carried


def empty_state(count_q, heads_here, head_width):
    return (
        jnp.full((count_q, heads_here), NEGATIVE, jnp.float32),
        jnp.zeros((count_q, heads_here), jnp.float32),
        jnp.zeros((count_q, heads_here, head_width), jnp.float32),
    )


def finish(carried):
    maxima, totals, running = carried
    return (running / totals[:, :, None]).reshape(running.shape[0], -1).astype(jnp.bfloat16)


def on_device(
    tokens,
    block_order,
    request_lengths,
    enc_lengths,
    w_qkv,
    w_out,
    enc_kv,
    w_cq,
    w_co,
    w_up,
    w_down,
    w_next,
):
    rows_here = tokens.shape[0]
    model_width = tokens.shape[1]
    group_size = lax.axis_size("head")
    cycle_size = lax.axis_size("blk")
    block_rows = rows_here * group_size
    halfway = block_rows // 2
    group_width = w_qkv.shape[2]
    head_width = model_width // HEADS
    group_heads = group_width // head_width
    gathered = lax.all_gather(tokens, "head", axis=0, tiled=True)
    projected = jnp.einsum(
        "td,cde->cte", gathered, w_qkv, preferred_element_type=jnp.float32
    ).astype(jnp.bfloat16)
    cycle_index = lax.axis_index("blk")
    block_start = cycle_index * block_rows
    query_places = position_of(
        block_order, block_start + jnp.arange(block_rows, dtype=jnp.int32), halfway
    )
    query_groups = group_of(query_places, request_lengths)
    queries = projected[0].reshape(block_rows, group_heads, head_width)
    start_state = empty_state(block_rows, group_heads, head_width)
    slots = jnp.arange(2 * cycle_size, dtype=jnp.int32)
    holders = jnp.sum(jnp.where(block_order[:, None] == slots[None, :], slots[:, None], 0), axis=0)
    start_carry = (start_state, jnp.zeros((1,), jnp.bfloat16))
    shards = (
        lax.all_gather(projected[1], "blk", axis=0, tiled=True),
        lax.all_gather(projected[2], "blk", axis=0, tiled=True),
    )
    shard_length = shards[0].shape[0]
    key_places = position_of(block_order, jnp.arange(shard_length, dtype=jnp.int32), halfway)
    key_groups = group_of(key_places, request_lengths)
    final_state = sweep(
        start_carry[0],
        queries,
        shards[0],
        shards[1],
        key_places,
        key_groups,
        query_places,
        query_groups,
    )
    attended = finish(final_state)
    pair = lax.dynamic_slice_in_dim(block_order, 2 * cycle_index, 2, 0)
    targets = pair // 2
    halves = projected[1:].reshape(2, 2, halfway, group_width)
    cycle_slots = jnp.arange(cycle_size, dtype=jnp.int32)
    outgoing = jnp.where(
        (cycle_slots == targets[0])[None, :, None, None],
        halves[:, 0][:, None],
        jnp.where(
            (cycle_slots == targets[1])[None, :, None, None],
            halves[:, 1][:, None],
            jnp.zeros((), jnp.bfloat16),
        ),
    )
    incoming = lax.all_to_all(outgoing, "blk", split_axis=1, concat_axis=1, tiled=True)
    first_source = lax.dynamic_index_in_dim(holders, 2 * cycle_index, 0, keepdims=False) // 2
    second_source = lax.dynamic_index_in_dim(holders, 2 * cycle_index + 1, 0, keepdims=False) // 2
    cache = jnp.concatenate(
        [
            lax.dynamic_index_in_dim(incoming, first_source, 1, keepdims=False),
            lax.dynamic_index_in_dim(incoming, second_source, 1, keepdims=False),
        ],
        axis=1,
    )
    mixed = lax.psum_scatter(
        jnp.dot(attended, w_out, preferred_element_type=jnp.float32),
        "head",
        scatter_dimension=0,
        tiled=True,
    )
    hidden = normalize(mixed + tokens.astype(jnp.float32))
    hidden_b = hidden.astype(jnp.bfloat16)
    member = lax.axis_index("head")
    own_places = lax.dynamic_slice_in_dim(query_places, member * rows_here, rows_here, 0)
    own_groups = group_of(own_places, request_lengths)
    cross_query = jnp.dot(hidden_b, w_cq, preferred_element_type=jnp.float32).astype(jnp.bfloat16)
    cross_split = cross_query.reshape(rows_here, HEADS, head_width)
    widened = lax.all_gather(enc_kv, "head", axis=2, tiled=True)
    shards = lax.all_gather(widened, "blk", axis=1, tiled=True)
    shard_length = shards.shape[1]
    encoder_groups = group_of(jnp.arange(shard_length, dtype=jnp.int32), enc_lengths)
    crossed = finish(
        sweep(
            empty_state(rows_here, HEADS, head_width),
            cross_split,
            shards[0],
            shards[1],
            None,
            encoder_groups,
            None,
            own_groups,
        )
    )
    summed = jnp.dot(crossed, w_co, preferred_element_type=jnp.float32)
    second = normalize(summed + hidden)
    second_b = second.astype(jnp.bfloat16)
    inner = jax.nn.gelu(
        jnp.dot(second_b, w_up, preferred_element_type=jnp.float32), approximate=False
    ).astype(jnp.bfloat16)
    output = normalize(jnp.dot(inner, w_down, preferred_element_type=jnp.float32) + second)
    output_b = output.astype(jnp.bfloat16)
    block_output = lax.all_gather(output_b, "head", axis=0, tiled=True)
    next_qkv = jnp.einsum("td,cde->cte", block_output, w_next, preferred_element_type=jnp.float32)
    return (output, cache, next_qkv)


def solution(mesh):
    in_specs = (
        P(("blk", "head"), None),
        P(),
        P(),
        P(),
        P(None, None, "head"),
        P("head", None),
        P(None, "blk", "head"),
        P(),
        P(),
        P(),
        P(),
        P(None, None, "head"),
    )
    out_specs = (P(("blk", "head"), None), P(None, "blk", "head"), P(None, "blk", "head"))
    return jax.shard_map(
        on_device, mesh=mesh, in_specs=in_specs, out_specs=out_specs, check_vma=False
    )
```

profile of v0, /device:TPU:1, one launch (start us, length us, event | category | flops | bytes accessed | tf_op | source)
XLA Modules:
  0.0 678.4 jit_solution(2549490070128636175)
XLA Ops:
  7.2 10.7 %all_gather.18 = bf16[384,1024]{1,0:T(8,128)(2,1)S(1)} all-gather(bf16[96,1024]{1,0:T(8,128)(2,1)} %param.14), channel_id=1, replica_groups=mesh['blk'=32,'head'=4] {'head'}, dimensions={0}, use_global_device_ids=true | all-gather | bytes 983040 | tf_op jit(solution)/shard_map/all_gather | solution.py:118
  25.4 97.8 %all-gather.8.cloned.1.call-done = bf16[1,12288,256]{1,2,0:T(8,128)(2,1)} async-done(((bf16[1,384,256]{1,2,0:T(8,128)(2,1)}), bf16[1,12288,256]{1,2,0:T(8,128)(2,1)}) %all-gather.8.cloned.1.call-update) | async-done | bytes 6291472 | tf_op jit(solution)/shard_map/all_gather | solution.py:134
  123.3 8.7 %copy.36 = bf16[1,12288,256]{2,1,0:T(8,128)(2,1)} copy(bf16[1,12288,256]{1,2,0:T(8,128)(2,1)} %all-gather.8.cloned.1.call-done) | data formatting | bytes 12582912 | tf_op jit(solution)/shard_map/all_gather | solution.py:134
  132.0 92.0 %all-gather.10.cloned.1.call-done = bf16[1,12288,256]{1,2,0:T(8,128)(2,1)} async-done(((bf16[1,384,256]{1,2,0:T(8,128)(2,1)}), bf16[1,12288,256]{1,2,0:T(8,128)(2,1)}) %all-gather.10.cloned.1.call-update) | async-done | bytes 6291472 | tf_op jit(solution)/shard_map/all_gather | solution.py:135
  224.0 8.6 %copy.37 = bf16[1,12288,256]{2,1,0:T(8,128)(2,1)} copy(bf16[1,12288,256]{1,2,0:T(8,128)(2,1)} %all-gather.10.cloned.1.call-done) | data formatting | bytes 12582912 | tf_op jit(solution)/shard_map/all_gather | solution.py:135
  232.6 196.6 %while.3 = (s32[]{:T(128)}, f32[384,4]{0,1:T(4,128)S(1)}, f32[384,4]{0,1:T(4,128)S(1)}, f32[384,4,64]{0,2,1:T(8,128)S(1)}, s32[6,2048]{1,0:T(8,128)}, /*index=5*...) while((s32[]{:T(128)}, f32[384,4]{0,1:T(4,128)S(1)}, ...), condition=%wide.region_11.12_spmd.clone, body=%wide.region_8.11_spmd.clone.sunk | while | flops 842571264 | bytes 52513932 | solution.py:76
  240.3 8.1 %fusion.171 = (f32[384,4]{0,1:T(4,128)S(1)}, f32[4,2048,384]{2,1,0:T(8,128)}) fusion(pred[384,2048]{0,1:T(8,128)(4,1)S(1)} %compare_and_fusion.2, bf16[2048,4,64]{0,2,1:T(8,128)(2,1)} %bitcast.119, bf16[384,4,64]{0,2,1:T(8,128)(2,1)S(1)} %get-tuple-element.334), kind=kOutput, calls=%fused_computation.4.clone.1 | convolution fusion | flops 412088832 | bytes 14620672 | tf_op jit(solution)/shard_map/while/body/eval_jaxpr/qhd,khd->qhk/dot_general | solution.py:37
  248.4 6.3 fusion.172
  257.1 8.3 %fusion.174 = f32[384,4,64]{0,2,1:T(8,128)S(1)} fusion(bf16[2048,4,64]{0,2,1:T(8,128)(2,1)} %bitcast.120, f32[4,2048,384]{2,1,0:T(8,128)} %get-tuple-element.295, f32[384,4]{0,1:T(4,128)S(1)} %select_maximum_fusion.2, pred[384,2048]{0,1:T(8,128)(4,1)S(1)} %compare_and_fusion.2, f32[384,4,64]{0,2,1:T(8,128)S(1)} %get-tuple-element.315, ...), kind=kOutput, calls=%fused_computation.9.clone.1 | convolution fusion | flops 415531008 | bytes 15216641 | tf_op jit(solution)/shard_map/while/body/eval_jaxpr/qhk,khd->qhd/dot_general | solution.py:44
  273.1 8.1 %fusion.171 = (f32[384,4]{0,1:T(4,128)S(1)}, f32[4,2048,384]{2,1,0:T(8,128)}) fusion(pred[384,2048]{0,1:T(8,128)(4,1)S(1)} %compare_and_fusion.2, bf16[2048,4,64]{0,2,1:T(8,128)(2,1)} %bitcast.119, bf16[384,4,64]{0,2,1:T(8,128)(2,1)S(1)} %get-tuple-element.334), kind=kOutput, calls=%fused_computation.4.clone.1 | convolution fusion | flops 412088832 | bytes 14620672 | tf_op jit(solution)/shard_map/while/body/eval_jaxpr/qhd,khd->qhk/dot_general | solution.py:37
  281.2 6.3 fusion.172
  289.8 8.3 %fusion.174 = f32[384,4,64]{0,2,1:T(8,128)S(1)} fusion(bf16[2048,4,64]{0,2,1:T(8,128)(2,1)} %bitcast.120, f32[4,2048,384]{2,1,0:T(8,128)} %get-tuple-element.295, f32[384,4]{0,1:T(4,128)S(1)} %select_maximum_fusion.2, pred[384,2048]{0,1:T(8,128)(4,1)S(1)} %compare_and_fusion.2, f32[384,4,64]{0,2,1:T(8,128)S(1)} %get-tuple-element.315, ...), kind=kOutput, calls=%fused_computation.9.clone.1 | convolution fusion | flops 415531008 | bytes 15216641 | tf_op jit(solution)/shard_map/while/body/eval_jaxpr/qhk,khd->qhd/dot_general | solution.py:44
  305.9 8.1 %fusion.171 = (f32[384,4]{0,1:T(4,128)S(1)}, f32[4,2048,384]{2,1,0:T(8,128)}) fusion(pred[384,2048]{0,1:T(8,128)(4,1)S(1)} %compare_and_fusion.2, bf16[2048,4,64]{0,2,1:T(8,128)(2,1)} %bitcast.119, bf16[384,4,64]{0,2,1:T(8,128)(2,1)S(1)} %get-tuple-element.334), kind=kOutput, calls=%fused_computation.4.clone.1 | convolution fusion | flops 412088832 | bytes 14620672 | tf_op jit(solution)/shard_map/while/body/eval_jaxpr/qhd,khd->qhk/dot_general | solution.py:37
  313.9 6.3 fusion.172
  322.6 8.3 %fusion.174 = f32[384,4,64]{0,2,1:T(8,128)S(1)} fusion(bf16[2048,4,64]{0,2,1:T(8,128)(2,1)} %bitcast.120, f32[4,2048,384]{2,1,0:T(8,128)} %get-tuple-element.295, f32[384,4]{0,1:T(4,128)S(1)} %select_maximum_fusion.2, pred[384,2048]{0,1:T(8,128)(4,1)S(1)} %compare_and_fusion.2, f32[384,4,64]{0,2,1:T(8,128)S(1)} %get-tuple-element.315, ...), kind=kOutput, calls=%fused_computation.9.clone.1 | convolution fusion | flops 415531008 | bytes 15216641 | tf_op jit(solution)/shard_map/while/body/eval_jaxpr/qhk,khd->qhd/dot_general | solution.py:44
  338.6 8.1 %fusion.171 = (f32[384,4]{0,1:T(4,128)S(1)}, f32[4,2048,384]{2,1,0:T(8,128)}) fusion(pred[384,2048]{0,1:T(8,128)(4,1)S(1)} %compare_and_fusion.2, bf16[2048,4,64]{0,2,1:T(8,128)(2,1)} %bitcast.119, bf16[384,4,64]{0,2,1:T(8,128)(2,1)S(1)} %get-tuple-element.334), kind=kOutput, calls=%fused_computation.4.clone.1 | convolution fusion | flops 412088832 | bytes 14620672 | tf_op jit(solution)/shard_map/while/body/eval_jaxpr/qhd,khd->qhk/dot_general | solution.py:37
  346.7 6.3 fusion.172
  355.4 8.3 %fusion.174 = f32[384,4,64]{0,2,1:T(8,128)S(1)} fusion(bf16[2048,4,64]{0,2,1:T(8,128)(2,1)} %bitcast.120, f32[4,2048,384]{2,1,0:T(8,128)} %get-tuple-element.295, f32[384,4]{0,1:T(4,128)S(1)} %select_maximum_fusion.2, pred[384,2048]{0,1:T(8,128)(4,1)S(1)} %compare_and_fusion.2, f32[384,4,64]{0,2,1:T(8,128)S(1)} %get-tuple-element.315, ...), kind=kOutput, calls=%fused_computation.9.clone.1 | convolution fusion | flops 415531008 | bytes 15216641 | tf_op jit(solution)/shard_map/while/body/eval_jaxpr/qhk,khd->qhd/dot_general | solution.py:44
  371.4 8.1 %fusion.171 = (f32[384,4]{0,1:T(4,128)S(1)}, f32[4,2048,384]{2,1,0:T(8,128)}) fusion(pred[384,2048]{0,1:T(8,128)(4,1)S(1)} %compare_and_fusion.2, bf16[2048,4,64]{0,2,1:T(8,128)(2,1)} %bitcast.119, bf16[384,4,64]{0,2,1:T(8,128)(2,1)S(1)} %get-tuple-element.334), kind=kOutput, calls=%fused_computation.4.clone.1 | convolution fusion | flops 412088832 | bytes 14620672 | tf_op jit(solution)/shard_map/while/body/eval_jaxpr/qhd,khd->qhk/dot_general | solution.py:37
  379.5 6.3 fusion.172
  388.1 8.3 %fusion.174 = f32[384,4,64]{0,2,1:T(8,128)S(1)} fusion(bf16[2048,4,64]{0,2,1:T(8,128)(2,1)} %bitcast.120, f32[4,2048,384]{2,1,0:T(8,128)} %get-tuple-element.295, f32[384,4]{0,1:T(4,128)S(1)} %select_maximum_fusion.2, pred[384,2048]{0,1:T(8,128)(4,1)S(1)} %compare_and_fusion.2, f32[384,4,64]{0,2,1:T(8,128)S(1)} %get-tuple-element.315, ...), kind=kOutput, calls=%fused_computation.9.clone.1 | convolution fusion | flops 415531008 | bytes 15216641 | tf_op jit(solution)/shard_map/while/body/eval_jaxpr/qhk,khd->qhd/dot_general | solution.py:44
  404.2 8.1 %fusion.171 = (f32[384,4]{0,1:T(4,128)S(1)}, f32[4,2048,384]{2,1,0:T(8,128)}) fusion(pred[384,2048]{0,1:T(8,128)(4,1)S(1)} %compare_and_fusion.2, bf16[2048,4,64]{0,2,1:T(8,128)(2,1)} %bitcast.119, bf16[384,4,64]{0,2,1:T(8,128)(2,1)S(1)} %get-tuple-element.334), kind=kOutput, calls=%fused_computation.4.clone.1 | convolution fusion | flops 412088832 | bytes 14620672 | tf_op jit(solution)/shard_map/while/body/eval_jaxpr/qhd,khd->qhk/dot_general | solution.py:37
  412.2 6.3 fusion.172
  420.9 8.3 %fusion.174 = f32[384,4,64]{0,2,1:T(8,128)S(1)} fusion(bf16[2048,4,64]{0,2,1:T(8,128)(2,1)} %bitcast.120, f32[4,2048,384]{2,1,0:T(8,128)} %get-tuple-element.295, f32[384,4]{0,1:T(4,128)S(1)} %select_maximum_fusion.2, pred[384,2048]{0,1:T(8,128)(4,1)S(1)} %compare_and_fusion.2, f32[384,4,64]{0,2,1:T(8,128)S(1)} %get-tuple-element.315, ...), kind=kOutput, calls=%fused_computation.9.clone.1 | convolution fusion | flops 415531008 | bytes 15216641 | tf_op jit(solution)/shard_map/while/body/eval_jaxpr/qhk,khd->qhd/dot_general | solution.py:44
  432.0 7.6 %all_gather.21 = bf16[2,64,1024]{2,1,0:T(8,128)(2,1)} all-gather(bf16[2,64,256]{2,1,0:T(8,128)(2,1)S(1)} %copy-done.5), channel_id=1, replica_groups=mesh['blk'=32,'head'=4] {'head'}, dimensions={2}, use_global_device_ids=true | all-gather | bytes 327680 | tf_op jit(solution)/shard_map/all_gather | solution.py:187
  457.0 85.6 %all-to-all-done = bf16[2,32,192,256]{3,2,0,1:T(8,128)(2,1)} async-done(((bf16[2,32,192,256]{3,2,0,1:T(8,128)(2,1)}), bf16[2,32,192,256]{3,2,0,1:T(8,128)(2,1)}, u32[]{:S(2)}, u32[]{:S(2)}) %all-to-all-start) | async-done | bytes 6291488 | tf_op jit(solution)/shard_map/all_to_all | solution.py:164
  549.3 62.4 %all-gather.6.cloned.1.call-done = bf16[2,2048,1024]{2,1,0:T(8,128)(2,1)} async-done(((bf16[2,64,1024]{2,1,0:T(8,128)(2,1)}), bf16[2,2048,1024]{2,1,0:T(8,128)(2,1)}) %all-gather.6.cloned.1.call-update) | async-done | bytes 8388624 | tf_op jit(solution)/shard_map/all_gather | solution.py:188
  617.6 6.5 copy.41
  633.2 6.5 copy.42
  639.7 9.5 %fusion.41 = bf16[96,16,64]{0,2,1:T(8,128)(2,1)S(1)} fusion(bf16[2048,16,64]{0,2,1:T(8,128)(2,1)} %bitcast.125, f32[16,96,2048]{2,1,0:T(8,128)} %copy-done.1, f32[96,16]{0,1:T(8,128)S(1)} %broadcast_maximum_fusion, pred[96,2048]{1,0:T(8,128)(4,1)S(1)} %broadcast_compare_fusion, f32[96,16]{0,1:T(8,128)S(1)} %get-tuple-element.203, ...), kind=kOutput, calls=%fused_computation.60 | convolution fusion | flops 415531008 | bytes 17188864 | tf_op jit(solution)/shard_map/while/body/eval_jaxpr/qhk,khd->qhd/dot_general | solution.py:44
  650.1 10.2 %fusion.142 = (f32[96]{0:T(128)S(1)}, f32[96,1024]{1,0:T(8,128)S(1)}) fusion(f32[96]{0:T(128)S(1)} %add_rsqrt_fusion.1, f32[96,1024]{1,0:T(8,128)S(1)} %get-tuple-element.211, f32[96]{0:T(128)S(1)} %broadcast_multiply_fusion.2, bf16[4096,1024]{1,0:T(8,128)(2,1)} %param.24, bf16[1024,4096]{1,0:T(8,128)(2,1)} %param.23), kind=kOutput, calls=%fused_computation.204 | convolution fusion | flops 1636859776 | bytes 17564800 | tf_op jit(solution)/shard_map/dot_general | solution.py:209
  661.4 8.7 %all_gather.23 = bf16[384,1024]{1,0:T(8,128)(2,1)S(1)} all-gather(bf16[96,1024]{1,0:T(8,128)(2,1)S(1)} %get-tuple-element.183), channel_id=1, replica_groups=mesh['blk'=32,'head'=4] {'head'}, dimensions={0}, use_global_device_ids=true | all-gather | bytes 983040 | tf_op jit(solution)/shard_map/all_gather | solution.py:211
  (134 shorter events, 108.1 us)
Async XLA Ops:
  7.2 642.1 %copy-start = (bf16[1024,1024]{1,0:T(8,128)(2,1)S(1)}, bf16[1024,1024]{1,0:T(8,128)(2,1)}, u32[]{:S(2)}) copy-start(bf16[1024,1024]{1,0:T(8,128)(2,1)} %param.22) | copy-start | bytes 6291460
  7.2 116.1 %all-gather.8.cloned.1.call-start = ((), (), s32[]{:S(2)}) async-start(), calls=%async_computation.4 | async-start | bytes 6488064 | tf_op jit(solution)/shard_map/all_gather | solution.py:134
  17.9 4.9 copy-start.8
  17.9 5.1 copy-start.6
  20.4 0.8 copy-start.4
  22.0 201.9 %all-gather.10.cloned.1.call-start = ((), (), s32[]{:S(2)}) async-start(), calls=%async_computation.5 | async-start | bytes 6488064 | tf_op jit(solution)/shard_map/all_gather | solution.py:135
  22.8 521.7 %reduce-scatter.2.cloned.1.call-start = ((), (), s32[]{:S(2)}) async-start(), calls=%async_computation.2 | async-start | bytes 1966080 | tf_op jit(solution)/shard_map/reduce_scatter | solution.py:174
  429.2 2.8 copy-start.5
  429.3 10.4 %slice-start = ((bf16[3,384,256]{1,2,0:T(8,128)(2,1)}), bf16[2,384,256]{1,2,0:T(8,128)(2,1)S(1)}, s32[]{:S(2)}) async-start(bf16[3,384,256]{1,2,0:T(8,128)(2,1)} %copy-done.4), calls=%async_computation.6 | async-start | bytes 786432 | tf_op jit(solution)/shard_map/slice | solution.py:153
  432.0 179.7 %all-gather.6.cloned.1.call-start = ((), (), s32[]{:S(2)}) async-start(), calls=%async_computation.3 | async-start | bytes 8650752 | tf_op jit(solution)/shard_map/all_gather | solution.py:188
  445.2 11.3 %copy-start.9 = (s32[9]{0:T(128)S(1)}, s32[9]{0:T(128)}, u32[]{:S(2)}) copy-start(s32[9]{0:T(128)} %param.17) | copy-start | bytes 112
  445.2 99.3 %copy-start.3 = (bf16[96,1024]{1,0:T(8,128)(2,1)S(1)}, bf16[96,1024]{1,0:T(8,128)(2,1)}, u32[]{:S(2)}) copy-start(bf16[96,1024]{1,0:T(8,128)(2,1)} %param.14) | copy-start | bytes 589828
  445.2 97.5 %all-to-all-start = ((bf16[2,32,192,256]{3,2,0,1:T(8,128)(2,1)}), bf16[2,32,192,256]{3,2,0,1:T(8,128)(2,1)}, u32[]{:S(2)}, u32[]{:S(2)}) async-start(bf16[2,32,192,256]{3,2,0,1:T(8,128)(2,1)} %select_select_fusion), calls=%async_computation.1 | async-start | bytes 12582912 | tf_op jit(solution)/shard_map/all_to_all | solution.py:164
  628.7 4.6 copy-start.1
  639.7 9.5 %copy-start.2 = (f32[96,1024]{1,0:T(8,128)S(1)}, f32[96,1024]{1,0:T(8,128)}, u32[]{:S(2)}) copy-start(f32[96,1024]{1,0:T(8,128)} %reduce-scatter.2.cloned.1.call-done) | copy-start | bytes 1179652
  660.3 9.8 %copy-start.7 = (bf16[3,1024,256]{2,1,0:T(8,128)(2,1)S(1)}, bf16[3,1024,256]{2,1,0:T(8,128)(2,1)}, u32[]{:S(2)}) copy-start(bf16[3,1024,256]{2,1,0:T(8,128)(2,1)} %param.25) | copy-start | bytes 4718596
Sparse Core Ops, SparseCore 0:
  22.2 101.0 all-gather.7
  126.6 97.2 all-gather.9
  432.1 22.4 reduce-scatter.1
  457.6 154.0 all-gather.5
where the time goes:
time: 681 us; the launch traced here: 678 us
  waiting for transfers between devices  339 us (50%)
  matrix products  132 us (19%)
  local copies, waits for them, and re-layouts  94.2 us (14%)
  other arithmetic  61.5 us (9%)
  blocking collectives  27.1 us (4%)
  between operations  19.3 us (3%)
    all_gather x1, waiting for transfers between devices, on_device(): lax.all_gather(projected[1], 'blk', axis=0, tiled=True)  97.8 us
    all_gather x1, waiting for transfers between devices, on_device(): lax.all_gather(projected[2], 'blk', axis=0, tiled=True)  92 us
    all_to_all x1, waiting for transfers between devices, on_device(): lax.all_to_all(outgoing, 'blk', split_axis=1, concat_axis=1, tiled=True)  85.6 us
    all_gather x1, waiting for transfers between devices, on_device(): shards = lax.all_gather(widened, 'blk', axis=1, tiled=True)  62.4 us
    dot_general x7, matrix products, online_update(): jnp.einsum('qhk,khd->qhd', weights.astype(jnp.bfloat16), value_split, pre...  59.2 us
    dot_general x7, matrix products, online_update(): jnp.einsum('qhd,khd->qhk', queries, key_split, preferred_element_type=jnp...  52.9 us
    dynamic_slice x24, local copies, waits for them, and re-layouts, sweep(): lax.scan(advance, carried, (key_blocks, value_blocks, place_blocks, group...  51.5 us
    reduce_sum x7, other arithmetic, online_update(): totals = totals * factor + jnp.sum(weights, axis=2)  40.9 us
  transfers between devices with their start and end apart: 5, of which 4 were waited for; matrix products, arithmetic and copies ran while one was open for 4% of the time, Pallas kernels for 0%

commit v1 on v0

--- a/solution.py
+++ b/solution.py
@@ -8,6 +8,13 @@
 NEGATIVE = -1e30
 SCALING = 0.125
 EPSILON = 1e-05
+
+
+def all_by_exchange(shard, mesh_axis, along):
+    size = lax.axis_size(mesh_axis)
+    tiles = jnp.stack([shard for _ in range(size)])
+    tiles = lax.all_to_all(tiles, mesh_axis, split_axis=0, concat_axis=0)
+    return jnp.concatenate(tiles, axis=along)
 
 
 def normalize(matrix):
@@ -131,7 +138,7 @@
     holders = jnp.sum(jnp.where(block_order[:, None] == slots[None, :], slots[:, None], 0), axis=0)
     start_carry = (start_state, jnp.zeros((1,), jnp.bfloat16))
     shards = (
-        lax.all_gather(projected[1], "blk", axis=0, tiled=True),
+        all_by_exchange(projected[1], "blk", 0),
         lax.all_gather(projected[2], "blk", axis=0, tiled=True),
     )
     shard_length = shards[0].shape[0]

time: 681 us -> 643 us (0.944)
  waiting for transfers between devices: 339 us -> 296 us
  starting transfers between devices: 5.43 us -> 15.9 us
    all_gather x1 -> x0, waiting for transfers between devices: 97.8 us -> none  [on_device(): lax.all_gather(projected[1], 'blk', axis=0, tiled=True)]
    all_gather x1, waiting for transfers between devices: 92 us -> 147 us  [on_device(): lax.all_gather(projected[2], 'blk', axis=0, tiled=True)]
    all_to_all x0 -> x1, starting transfers between devices: none -> 10.3 us  [all_by_exchange(): tiles = lax.all_to_all(tiles, mesh_axis, split_axis=0, concat_axis=0)]
    all_gather x1 -> x0, local copies, waits for them, and re-layouts: 8.68 us -> none  [on_device(): lax.all_gather(projected[1], 'blk', axis=0, tiled=True)]
  transfers between devices with their start and end apart: 5 -> 5, of which waited for: 4 -> 3; matrix products, arithmetic and copies ran while one was open for 4% -> 4% of each run, Pallas kernels for 0% -> 0%
where the time goes in v1:
time: 643 us; the launch traced here: 641 us
  waiting for transfers between devices  296 us (46%)
  matrix products  132 us (21%)
  local copies, waits for them, and re-layouts  89 us (14%)
  other arithmetic  61.5 us (10%)
  blocking collectives  27.1 us (4%)
  between operations  19.3 us (3%)
  starting transfers between devices  15.9 us (2%)
    all_gather x1, waiting for transfers between devices, on_device(): lax.all_gather(projected[2], 'blk', axis=0, tiled=True)  147 us
    all_to_all x1, waiting for transfers between devices, on_device(): lax.all_to_all(outgoing, 'blk', split_axis=1, concat_axis=1, tiled=True)  85.5 us
    all_gather x1, waiting for transfers between devices, on_device(): shards = lax.all_gather(widened, 'blk', axis=1, tiled=True)  62.8 us
    dot_general x7, matrix products, online_update(): jnp.einsum('qhk,khd->qhd', weights.astype(jnp.bfloat16), value_split, pre...  59.2 us
    dot_general x7, matrix products, online_update(): jnp.einsum('qhd,khd->qhk', queries, key_split, preferred_element_type=jnp...  52.9 us
    dynamic_slice x24, local copies, waits for them, and re-layouts, sweep(): lax.scan(advance, carried, (key_blocks, value_blocks, place_blocks, group...  51.5 us
    reduce_sum x7, other arithmetic, online_update(): totals = totals * factor + jnp.sum(weights, axis=2)  40.9 us
  transfers between devices with their start and end apart: 5, of which 3 were waited for; matrix products, arithmetic and copies ran while one was open for 4% of the time, Pallas kernels for 0%

profile of v1, /device:TPU:1, one launch (start us, length us, event | category | flops | bytes accessed | tf_op | source)
XLA Modules:
  0.0 640.7 jit_solution(8386161504564473757)
XLA Ops:
  7.2 10.7 %all_gather.15 = bf16[384,1024]{1,0:T(8,128)(2,1)S(1)} all-gather(bf16[96,1024]{1,0:T(8,128)(2,1)} %param.14), channel_id=1, replica_groups=mesh['blk'=32,'head'=4] {'head'}, dimensions={0}, use_global_device_ids=true | all-gather | bytes 983040 | tf_op jit(solution)/shard_map/all_gather | solution.py:125
  25.5 10.3 %all-to-all-start = ((bf16[32,384,256]{2,1,0:T(8,128)(2,1)}), bf16[32,384,256]{2,1,0:T(8,128)(2,1)}, u32[]{:S(2)}, u32[]{:S(2)}) async-start(bf16[32,384,256]{2,1,0:T(8,128)(2,1)} %stack.3), calls=%async_computation | async-start | bytes 12582912 | tf_op jit(solution)/shard_map/all_to_all | solution.py:16
  38.6 147.4 %all-gather.6.cloned.1.call-done = bf16[1,12288,256]{1,2,0:T(8,128)(2,1)} async-done(((bf16[1,384,256]{1,2,0:T(8,128)(2,1)}), bf16[1,12288,256]{1,2,0:T(8,128)(2,1)}) %all-gather.6.cloned.1.call-update) | async-done | bytes 6291472 | tf_op jit(solution)/shard_map/all_gather | solution.py:142
  186.0 8.6 %copy.37 = bf16[1,12288,256]{2,1,0:T(8,128)(2,1)} copy(bf16[1,12288,256]{1,2,0:T(8,128)(2,1)} %all-gather.6.cloned.1.call-done) | data formatting | bytes 12582912 | tf_op jit(solution)/shard_map/all_gather | solution.py:142
  194.6 196.6 %while.3 = (s32[]{:T(128)}, f32[384,4]{0,1:T(4,128)S(1)}, f32[384,4]{0,1:T(4,128)S(1)}, f32[384,4,64]{0,2,1:T(8,128)S(1)}, s32[6,2048]{1,0:T(8,128)}, /*index=5*...) while((s32[]{:T(128)}, f32[384,4]{0,1:T(4,128)S(1)}, ...), condition=%wide.region_11.12_spmd.clone, body=%wide.region_8.11_spmd.clone.sunk | while | flops 842571264 | bytes 52513932 | solution.py:83
  202.4 8.1 %fusion.171 = (f32[384,4]{0,1:T(4,128)S(1)}, f32[4,2048,384]{2,1,0:T(8,128)}) fusion(pred[384,2048]{0,1:T(8,128)(4,1)S(1)} %compare_and_fusion.2, bf16[2048,4,64]{0,2,1:T(8,128)(2,1)} %bitcast.121, bf16[384,4,64]{0,2,1:T(8,128)(2,1)S(1)} %get-tuple-element.334), kind=kOutput, calls=%fused_computation.4.clone.1 | convolution fusion | flops 412088832 | bytes 14620672 | tf_op jit(solution)/shard_map/while/body/eval_jaxpr/qhd,khd->qhk/dot_general | solution.py:44
  210.4 6.3 fusion.172
  219.1 8.3 %fusion.174 = f32[384,4,64]{0,2,1:T(8,128)S(1)} fusion(bf16[2048,4,64]{0,2,1:T(8,128)(2,1)} %bitcast.122, f32[4,2048,384]{2,1,0:T(8,128)} %get-tuple-element.295, f32[384,4]{0,1:T(4,128)S(1)} %select_maximum_fusion.2, pred[384,2048]{0,1:T(8,128)(4,1)S(1)} %compare_and_fusion.2, f32[384,4,64]{0,2,1:T(8,128)S(1)} %get-tuple-element.315, ...), kind=kOutput, calls=%fused_computation.9.clone.1 | convolution fusion | flops 415531008 | bytes 15216641 | tf_op jit(solution)/shard_map/while/body/eval_jaxpr/qhk,khd->qhd/dot_general | solution.py:51
  235.1 8.1 %fusion.171 = (f32[384,4]{0,1:T(4,128)S(1)}, f32[4,2048,384]{2,1,0:T(8,128)}) fusion(pred[384,2048]{0,1:T(8,128)(4,1)S(1)} %compare_and_fusion.2, bf16[2048,4,64]{0,2,1:T(8,128)(2,1)} %bitcast.121, bf16[384,4,64]{0,2,1:T(8,128)(2,1)S(1)} %get-tuple-element.334), kind=kOutput, calls=%fused_computation.4.clone.1 | convolution fusion | flops 412088832 | bytes 14620672 | tf_op jit(solution)/shard_map/while/body/eval_jaxpr/qhd,khd->qhk/dot_general | solution.py:44
  243.2 6.3 fusion.172
  251.9 8.3 %fusion.174 = f32[384,4,64]{0,2,1:T(8,128)S(1)} fusion(bf16[2048,4,64]{0,2,1:T(8,128)(2,1)} %bitcast.122, f32[4,2048,384]{2,1,0:T(8,128)} %get-tuple-element.295, f32[384,4]{0,1:T(4,128)S(1)} %select_maximum_fusion.2, pred[384,2048]{0,1:T(8,128)(4,1)S(1)} %compare_and_fusion.2, f32[384,4,64]{0,2,1:T(8,128)S(1)} %get-tuple-element.315, ...), kind=kOutput, calls=%fused_computation.9.clone.1 | convolution fusion | flops 415531008 | bytes 15216641 | tf_op jit(solution)/shard_map/while/body/eval_jaxpr/qhk,khd->qhd/dot_general | solution.py:51
  267.9 8.1 %fusion.171 = (f32[384,4]{0,1:T(4,128)S(1)}, f32[4,2048,384]{2,1,0:T(8,128)}) fusion(pred[384,2048]{0,1:T(8,128)(4,1)S(1)} %compare_and_fusion.2, bf16[2048,4,64]{0,2,1:T(8,128)(2,1)} %bitcast.121, bf16[384,4,64]{0,2,1:T(8,128)(2,1)S(1)} %get-tuple-element.334), kind=kOutput, calls=%fused_computation.4.clone.1 | convolution fusion | flops 412088832 | bytes 14620672 | tf_op jit(solution)/shard_map/while/body/eval_jaxpr/qhd,khd->qhk/dot_general | solution.py:44
  276.0 6.3 fusion.172
  284.6 8.3 %fusion.174 = f32[384,4,64]{0,2,1:T(8,128)S(1)} fusion(bf16[2048,4,64]{0,2,1:T(8,128)(2,1)} %bitcast.122, f32[4,2048,384]{2,1,0:T(8,128)} %get-tuple-element.295, f32[384,4]{0,1:T(4,128)S(1)} %select_maximum_fusion.2, pred[384,2048]{0,1:T(8,128)(4,1)S(1)} %compare_and_fusion.2, f32[384,4,64]{0,2,1:T(8,128)S(1)} %get-tuple-element.315, ...), kind=kOutput, calls=%fused_computation.9.clone.1 | convolution fusion | flops 415531008 | bytes 15216641 | tf_op jit(solution)/shard_map/while/body/eval_jaxpr/qhk,khd->qhd/dot_general | solution.py:51
  300.7 8.1 %fusion.171 = (f32[384,4]{0,1:T(4,128)S(1)}, f32[4,2048,384]{2,1,0:T(8,128)}) fusion(pred[384,2048]{0,1:T(8,128)(4,1)S(1)} %compare_and_fusion.2, bf16[2048,4,64]{0,2,1:T(8,128)(2,1)} %bitcast.121, bf16[384,4,64]{0,2,1:T(8,128)(2,1)S(1)} %get-tuple-element.334), kind=kOutput, calls=%fused_computation.4.clone.1 | convolution fusion | flops 412088832 | bytes 14620672 | tf_op jit(solution)/shard_map/while/body/eval_jaxpr/qhd,khd->qhk/dot_general | solution.py:44
  308.7 6.3 fusion.172
  317.4 8.3 %fusion.174 = f32[384,4,64]{0,2,1:T(8,128)S(1)} fusion(bf16[2048,4,64]{0,2,1:T(8,128)(2,1)} %bitcast.122, f32[4,2048,384]{2,1,0:T(8,128)} %get-tuple-element.295, f32[384,4]{0,1:T(4,128)S(1)} %select_maximum_fusion.2, pred[384,2048]{0,1:T(8,128)(4,1)S(1)} %compare_and_fusion.2, f32[384,4,64]{0,2,1:T(8,128)S(1)} %get-tuple-element.315, ...), kind=kOutput, calls=%fused_computation.9.clone.1 | convolution fusion | flops 415531008 | bytes 15216641 | tf_op jit(solution)/shard_map/while/body/eval_jaxpr/qhk,khd->qhd/dot_general | solution.py:51
  333.4 8.1 %fusion.171 = (f32[384,4]{0,1:T(4,128)S(1)}, f32[4,2048,384]{2,1,0:T(8,128)}) fusion(pred[384,2048]{0,1:T(8,128)(4,1)S(1)} %compare_and_fusion.2, bf16[2048,4,64]{0,2,1:T(8,128)(2,1)} %bitcast.121, bf16[384,4,64]{0,2,1:T(8,128)(2,1)S(1)} %get-tuple-element.334), kind=kOutput, calls=%fused_computation.4.clone.1 | convolution fusion | flops 412088832 | bytes 14620672 | tf_op jit(solution)/shard_map/while/body/eval_jaxpr/qhd,khd->qhk/dot_general | solution.py:44
  341.5 6.3 fusion.172
  350.2 8.3 %fusion.174 = f32[384,4,64]{0,2,1:T(8,128)S(1)} fusion(bf16[2048,4,64]{0,2,1:T(8,128)(2,1)} %bitcast.122, f32[4,2048,384]{2,1,0:T(8,128)} %get-tuple-element.295, f32[384,4]{0,1:T(4,128)S(1)} %select_maximum_fusion.2, pred[384,2048]{0,1:T(8,128)(4,1)S(1)} %compare_and_fusion.2, f32[384,4,64]{0,2,1:T(8,128)S(1)} %get-tuple-element.315, ...), kind=kOutput, calls=%fused_computation.9.clone.1 | convolution fusion | flops 415531008 | bytes 15216641 | tf_op jit(solution)/shard_map/while/body/eval_jaxpr/qhk,khd->qhd/dot_general | solution.py:51
  366.2 8.1 %fusion.171 = (f32[384,4]{0,1:T(4,128)S(1)}, f32[4,2048,384]{2,1,0:T(8,128)}) fusion(pred[384,2048]{0,1:T(8,128)(4,1)S(1)} %compare_and_fusion.2, bf16[2048,4,64]{0,2,1:T(8,128)(2,1)} %bitcast.121, bf16[384,4,64]{0,2,1:T(8,128)(2,1)S(1)} %get-tuple-element.334), kind=kOutput, calls=%fused_computation.4.clone.1 | convolution fusion | flops 412088832 | bytes 14620672 | tf_op jit(solution)/shard_map/while/body/eval_jaxpr/qhd,khd->qhk/dot_general | solution.py:44
  374.2 6.3 fusion.172
  382.9 8.3 %fusion.174 = f32[384,4,64]{0,2,1:T(8,128)S(1)} fusion(bf16[2048,4,64]{0,2,1:T(8,128)(2,1)} %bitcast.122, f32[4,2048,384]{2,1,0:T(8,128)} %get-tuple-element.295, f32[384,4]{0,1:T(4,128)S(1)} %select_maximum_fusion.2, pred[384,2048]{0,1:T(8,128)(4,1)S(1)} %compare_and_fusion.2, f32[384,4,64]{0,2,1:T(8,128)S(1)} %get-tuple-element.315, ...), kind=kOutput, calls=%fused_computation.9.clone.1 | convolution fusion | flops 415531008 | bytes 15216641 | tf_op jit(solution)/shard_map/while/body/eval_jaxpr/qhk,khd->qhd/dot_general | solution.py:51
  394.0 7.6 %all_gather.17 = bf16[2,64,1024]{2,1,0:T(8,128)(2,1)} all-gather(bf16[2,64,256]{2,1,0:T(8,128)(2,1)S(1)} %copy-done.5), channel_id=1, replica_groups=mesh['blk'=32,'head'=4] {'head'}, dimensions={2}, use_global_device_ids=true | all-gather | bytes 327680 | tf_op jit(solution)/shard_map/all_gather | solution.py:194
  419.0 85.5 %all-to-all-done.1 = bf16[2,32,192,256]{3,2,0,1:T(8,128)(2,1)} async-done(((bf16[2,32,192,256]{3,2,0,1:T(8,128)(2,1)}), bf16[2,32,192,256]{3,2,0,1:T(8,128)(2,1)}, u32[]{:S(2)}, u32[]{:S(2)}) %all-to-all-start.1) | async-done | bytes 6291488 | tf_op jit(solution)/shard_map/all_to_all | solution.py:171
  511.1 62.8 %all-gather.4.cloned.1.call-done = bf16[2,2048,1024]{2,1,0:T(8,128)(2,1)} async-done(((bf16[2,64,1024]{2,1,0:T(8,128)(2,1)}), bf16[2,2048,1024]{2,1,0:T(8,128)(2,1)}) %all-gather.4.cloned.1.call-update) | async-done | bytes 8388624 | tf_op jit(solution)/shard_map/all_gather | solution.py:195
  573.9 5.9 fusion.137
  579.8 6.5 %copy.41 = bf16[1,2048,1024]{1,2,0:T(8,128)(2,1)} copy(bf16[1,2048,1024]{2,1,0:T(8,128)(2,1)} %get-tuple-element.191) | data formatting | bytes 8388608 | tf_op jit(solution)/shard_map/slice | solution.py:202
  595.5 6.5 %copy.42 = bf16[1,2048,1024]{1,2,0:T(8,128)(2,1)} copy(bf16[1,2048,1024]{2,1,0:T(8,128)(2,1)} %get-tuple-element.192) | data formatting | bytes 8388608 | tf_op jit(solution)/shard_map/slice | solution.py:203
  602.0 9.5 %fusion.41 = bf16[96,16,64]{0,2,1:T(8,128)(2,1)S(1)} fusion(bf16[2048,16,64]{0,2,1:T(8,128)(2,1)} %bitcast.126, f32[16,96,2048]{2,1,0:T(8,128)} %copy-done.1, f32[96,16]{0,1:T(8,128)S(1)} %broadcast_maximum_fusion, pred[96,2048]{1,0:T(8,128)(4,1)S(1)} %broadcast_compare_fusion, f32[96,16]{0,1:T(8,128)S(1)} %get-tuple-element.203, ...), kind=kOutput, calls=%fused_computation.60 | convolution fusion | flops 415531008 | bytes 17188864 | tf_op jit(solution)/shard_map/while/body/eval_jaxpr/qhk,khd->qhd/dot_general | solution.py:51
  612.3 10.3 %fusion.142 = (f32[96]{0:T(128)S(1)}, f32[96,1024]{1,0:T(8,128)S(1)}) fusion(f32[96]{0:T(128)S(1)} %add_rsqrt_fusion.1, f32[96,1024]{1,0:T(8,128)S(1)} %get-tuple-element.211, f32[96]{0:T(128)S(1)} %broadcast_multiply_fusion.2, bf16[4096,1024]{1,0:T(8,128)(2,1)} %param.24, bf16[1024,4096]{1,0:T(8,128)(2,1)} %param.23), kind=kOutput, calls=%fused_computation.205 | convolution fusion | flops 1636859776 | bytes 17564800 | tf_op jit(solution)/shard_map/dot_general | solution.py:216
  623.7 8.7 %all_gather.19 = bf16[384,1024]{1,0:T(8,128)(2,1)S(1)} all-gather(bf16[96,1024]{1,0:T(8,128)(2,1)S(1)} %get-tuple-element.183), channel_id=1, replica_groups=mesh['blk'=32,'head'=4] {'head'}, dimensions={0}, use_global_device_ids=true | all-gather | bytes 983040 | tf_op jit(solution)/shard_map/all_gather | solution.py:218
  (134 shorter events, 105.1 us)
Async XLA Ops:
  7.2 604.3 %copy-start = (bf16[1024,1024]{1,0:T(8,128)(2,1)S(1)}, bf16[1024,1024]{1,0:T(8,128)(2,1)}, u32[]{:S(2)}) copy-start(bf16[1024,1024]{1,0:T(8,128)(2,1)} %param.22) | copy-start | bytes 6291460
  7.2 178.8 %all-gather.6.cloned.1.call-start = ((), (), s32[]{:S(2)}) async-start(), calls=%async_computation.5 | async-start | bytes 6488064 | tf_op jit(solution)/shard_map/all_gather | solution.py:142
  20.4 0.8 copy-start.4
  25.5 10.6 %copy-start.8 = (s32[9]{0:T(128)S(1)}, s32[9]{0:T(128)}, u32[]{:S(2)}) copy-start(s32[9]{0:T(128)} %param.16) | copy-start | bytes 112
  25.5 10.8 %copy-start.6 = (s32[64]{0:T(128)S(1)}, s32[64]{0:T(128)}, u32[]{:S(2)}) copy-start(s32[64]{0:T(128)} %param.15) | copy-start | bytes 772
  25.5 169.2 %all-to-all-start = ((bf16[32,384,256]{2,1,0:T(8,128)(2,1)}), bf16[32,384,256]{2,1,0:T(8,128)(2,1)}, u32[]{:S(2)}, u32[]{:S(2)}) async-start(bf16[32,384,256]{2,1,0:T(8,128)(2,1)} %stack.3), calls=%async_computation | async-start | bytes 12582912 | tf_op jit(solution)/shard_map/all_to_all | solution.py:16
  35.8 470.6 %reduce-scatter.2.cloned.1.call-start = ((), (), s32[]{:S(2)}) async-start(), calls=%async_computation.3 | async-start | bytes 1966080 | tf_op jit(solution)/shard_map/reduce_scatter | solution.py:181
  391.2 2.8 copy-start.5
  391.3 10.4 %slice-start = ((bf16[3,384,256]{1,2,0:T(8,128)(2,1)}), bf16[2,384,256]{1,2,0:T(8,128)(2,1)S(1)}, s32[]{:S(2)}) async-start(bf16[3,384,256]{1,2,0:T(8,128)(2,1)} %copy-done.4), calls=%async_computation.6 | async-start | bytes 786432 | tf_op jit(solution)/shard_map/slice | solution.py:160
  394.0 179.9 %all-gather.4.cloned.1.call-start = ((), (), s32[]{:S(2)}) async-start(), calls=%async_computation.4 | async-start | bytes 8650752 | tf_op jit(solution)/shard_map/all_gather | solution.py:195
  407.2 11.3 %copy-start.9 = (s32[9]{0:T(128)S(1)}, s32[9]{0:T(128)}, u32[]{:S(2)}) copy-start(s32[9]{0:T(128)} %param.17) | copy-start | bytes 112
  407.2 99.2 %copy-start.3 = (bf16[96,1024]{1,0:T(8,128)(2,1)S(1)}, bf16[96,1024]{1,0:T(8,128)(2,1)}, u32[]{:S(2)}) copy-start(bf16[96,1024]{1,0:T(8,128)(2,1)} %param.14) | copy-start | bytes 589828
  407.2 97.3 %all-to-all-start.1 = ((bf16[2,32,192,256]{3,2,0,1:T(8,128)(2,1)}), bf16[2,32,192,256]{3,2,0,1:T(8,128)(2,1)}, u32[]{:S(2)}, u32[]{:S(2)}) async-start(bf16[2,32,192,256]{3,2,0,1:T(8,128)(2,1)} %select_select_fusion), calls=%async_computation.2 | async-start | bytes 12582912 | tf_op jit(solution)/shard_map/all_to_all | solution.py:171
  590.9 4.6 copy-start.1
  602.0 9.5 %copy-start.2 = (f32[96,1024]{1,0:T(8,128)S(1)}, f32[96,1024]{1,0:T(8,128)}, u32[]{:S(2)}) copy-start(f32[96,1024]{1,0:T(8,128)} %reduce-scatter.2.cloned.1.call-done) | copy-start | bytes 1179652
  622.6 9.8 %copy-start.7 = (bf16[3,1024,256]{2,1,0:T(8,128)(2,1)S(1)}, bf16[3,1024,256]{2,1,0:T(8,128)(2,1)}, u32[]{:S(2)}) copy-start(bf16[3,1024,256]{2,1,0:T(8,128)(2,1)} %param.25) | copy-start | bytes 4718596
Sparse Core Ops, SparseCore 0:
  22.1 163.8 all-gather.5
  394.1 22.3 reduce-scatter.1
  419.7 154.2 all-gather.3
